TPU v7x, 512 devices: a whole 4x8x8 slice. The times are simulated.
512 devices in a mesh: layer: 16 (over x, z_hi, core), col: 32 (over z_lo, y).
Axes of the slice: x: 4, y: 8, z: 8 (z_hi: 2, z_lo: 4; z = z_hi * 4 + z_lo), core: 2. Of those that a mesh axis runs over, the one named last changes fastest.
Arguments:
- lower_panel: bfloat16 [16, 4096, 768], P('layer', 'col'), may hold values from -0.109375 to 0.109375
- upper_panel: bfloat16 [16, 768, 4096], P('layer', None, 'col'), may hold values from -6 to 6
- diag_inverse: bfloat16 [16, 1, 768, 768], P('layer'), may hold values from -1 to 2, as said below
- pivot_inverse: bfloat16 [4, 128, 128], replicated, may hold values from -0.1 to 0.1, as said below
- pattern: int32 [16, 2, 32], P('layer'), may hold values 0 or 1
- col_order: int32 [32], replicated, may hold values from 0 to 31, each once
- sep_blocks: int32 [4], replicated, may hold values from 0 to 31, as said below
Outputs:
- schur_top: bfloat16 [4096, 4096], P('layer', 'col')
Inputs may be any that keep to these rules, and one draw needn't show every extreme that they name: `diag_inverse`: each is the identity plus a full matrix of smaller entries. `pivot_inverse`: full matrices. `sep_blocks`: the 4 entries are distinct.
All inputs are finite; a program needn't handle non-finite values. No bound on the sum of `pattern` on one device may be relied on, other than what follows from the above.
Results may differ from a plain program's by a relative error of at most 0.0088.
Values may be sent and summed in bfloat16 or wider, within the bound.
No kernel may reach another device: no remote copies, remote signals or barrier semaphores. Data moves between devices by JAX's collectives and lax.ppermute only.
A program may use at most 64 MiB of HBM per device.

v0:
```python
import jax
import jax.numpy as jnp
from jax import lax
from jax.sharding import PartitionSpec as P

NB = 128


def from_partner(value, axis, distance):
    mask = 2**distance
    pairs = [(source, source ^ mask) for source in range(lax.axis_size(axis))]
    return lax.ppermute(value, axis, pairs)


def broadcast(x, axis, root):
    mine = lax.axis_index(axis) == root
    return lax.psum(jnp.where(mine, x, jnp.zeros_like(x)), axis)


def shards(lower_panel, upper_panel, diag_inverse, pivot_inverse, pattern, col_order, sep_blocks):
    supernodes = diag_inverse.shape[1]
    node_width = diag_inverse.shape[2]
    local_cols = upper_panel.shape[2]
    col_index = lax.axis_index("col")
    first_col = col_index * local_cols
    nblocks = col_order.shape[0]
    solved = jnp.einsum(
        "sab,sbc->sac",
        diag_inverse[0],
        upper_panel[0].reshape(supernodes, node_width, local_cols),
        preferred_element_type=jnp.float32,
    )
    right = solved.astype(jnp.bfloat16).reshape(supernodes * node_width, local_cols)
    row_flags = jnp.repeat(pattern[0, 0], NB).astype(jnp.float32)
    all_col_flags = jnp.repeat(pattern[0, 1], NB).astype(jnp.float32)
    col_flags = lax.dynamic_slice_in_dim(all_col_flags, first_col, local_cols)
    product = jnp.dot(
        lax.all_gather(lower_panel[0], "col", axis=0, tiled=True),
        right,
        preferred_element_type=jnp.float32,
    )
    current = (-product * row_flags[:, None] * col_flags[None, :]).astype(jnp.bfloat16)
    layer_count = lax.axis_size("layer")
    layer_index = lax.axis_index("layer")
    levels = layer_count.bit_length() - 1
    positions = jnp.arange(nblocks, dtype=jnp.int32)
    total_rows = current.shape[0]
    span_rows = total_rows // layer_count
    row_blocks = jnp.arange(total_rows, dtype=jnp.int32) // NB
    col_blocks = (first_col + jnp.arange(local_cols, dtype=jnp.int32)) // NB
    for level in range(levels):
        partner = from_partner(current, "layer", level)
        total = current.astype(jnp.float32) + partner.astype(jnp.float32)
        separator = sep_blocks[level]
        position = jnp.sum(jnp.where(col_order == separator, positions, 0))
        owner = position * NB // local_cols
        local_panel = total.astype(jnp.bfloat16)
        local_factor = jnp.dot(
            local_panel, pivot_inverse[level], preferred_element_type=jnp.float32
        ).astype(jnp.bfloat16)
        factor = broadcast(local_factor, "col", owner)
        upper_rows = lax.dynamic_slice_in_dim(total, separator * NB, NB, 0).astype(jnp.bfloat16)
        updated = total - jnp.dot(factor, upper_rows, preferred_element_type=jnp.float32)
        keep = (row_blocks != separator)[:, None] & (col_blocks != position)[None, :]
        current = jnp.where(keep, updated, jnp.zeros_like(updated)).astype(jnp.bfloat16)
    result = lax.dynamic_slice_in_dim(current, layer_index * span_rows, span_rows, 0)
    return result


def solution(mesh):
    in_specs = (
        P("layer", "col", None),
        P("layer", None, "col"),
        P("layer", None, None, None),
        P(),
        P("layer", None, None),
        P(),
        P(),
    )
    out_specs = P("layer", "col")
    return jax.shard_map(shards, mesh=mesh, in_specs=in_specs, out_specs=out_specs, check_vma=False)
```

profile of v0, /device:TPU:2, one launch (start us, length us, event | category | flops | bytes accessed | tf_op | source)
XLA Modules:
  0.0 1500.4 jit_solution(14784830018632039994)
XLA Ops:
  8.2 170.0 %all-gather.3.cloned.1.call-done = bf16[1,4096,768]{2,1,0:T(8,128)(2,1)} async-done(((bf16[1,128,768]{2,1,0:T(8,128)(2,1)}), bf16[1,4096,768]{2,1,0:T(8,128)(2,1)}) %all-gather.3.cloned.1.call-update) | async-done | bytes 6291472 | tf_op jit(solution)/shard_map/all_gather | solution.py:38
  178.2 5.8 fusion.24
  184.0 1.9 collective-permute-start
  186.6 3.1 fusion.63
  191.0 1.6 fusion.20
  193.9 1.6 convert_add_fusion.3
  195.5 304.2 %all-reduce.5.cloned.1.call-done = bf16[4096,128]{1,0:T(8,128)(2,1)} async-done(((bf16[4096,128]{1,0:T(8,128)(2,1)}), bf16[4096,128]{1,0:T(8,128)(2,1)}) %all-reduce.5.cloned.1.call-update) | async-done | bytes 1048592 | tf_op jit(solution)/shard_map/psum | solution.py:17
  499.7 2.4 fusion.17
  502.1 5.7 collective-permute-start.1
  509.1 15.5 %collective-permute-done.1 = bf16[4096,128]{0,1:T(8,128)(2,1)S(1)} collective-permute-done((bf16[4096,128]{0,1:T(8,128)(2,1)S(1)}, bf16[4096,128]{0,1:T(8,128)(2,1)S(1)}, u32[]{:S(2)}, u32[]{:S(2)}) %collective-permute-start.1) | collective-permute-done | bytes 1048608 | tf_op jit(solution)/shard_map/ppermute | solution.py:12
  524.6 1.6 fusion.21
  527.5 1.6 convert_add_fusion.2
  529.1 304.9 %all-reduce.7.cloned.1.call-done = bf16[4096,128]{1,0:T(8,128)(2,1)} async-done(((bf16[4096,128]{1,0:T(8,128)(2,1)}), bf16[4096,128]{1,0:T(8,128)(2,1)}) %all-reduce.7.cloned.1.call-update) | async-done | bytes 1048592 | tf_op jit(solution)/shard_map/psum | solution.py:17
  834.1 2.4 fusion.18
  836.5 2.5 collective-permute-start.2
  840.2 13.0 collective-permute-done.2
  856.1 1.6 convert_add_fusion.1
  857.7 303.8 %all-reduce.9.cloned.1.call-done = bf16[4096,128]{1,0:T(8,128)(2,1)} async-done(((bf16[4096,128]{1,0:T(8,128)(2,1)}), bf16[4096,128]{1,0:T(8,128)(2,1)}) %all-reduce.9.cloned.1.call-update) | async-done | bytes 1048592 | tf_op jit(solution)/shard_map/psum | solution.py:17
  1161.5 2.4 fusion.19
  1163.9 4.0 collective-permute-start.3
  1169.2 12.9 collective-permute-done.3
  1185.1 1.6 convert_add_fusion
  1186.7 303.8 %all-reduce.11.cloned.1.call-done = bf16[4096,128]{1,0:T(8,128)(2,1)} async-done(((bf16[4096,128]{1,0:T(8,128)(2,1)}), bf16[4096,128]{1,0:T(8,128)(2,1)}) %all-reduce.11.cloned.1.call-update) | async-done | bytes 1048592 | tf_op jit(solution)/shard_map/psum | solution.py:17
  1490.4 1.7 fusion.42
  (36 shorter events, 12.5 us)
Async XLA Ops:
  6.5 171.7 %copy-start = (bf16[1,1,768,768]{3,2,1,0:T(8,128)(2,1)S(1)}, bf16[1,1,768,768]{3,2,1,0:T(8,128)(2,1)}, u32[]{:S(2)}) copy-start(bf16[1,1,768,768]{3,2,1,0:T(8,128)(2,1)} %param.9) | copy-start | bytes 3538948
  6.5 171.6 %all-gather.3.cloned.1.call-start = ((), (), s32[]{:S(2)}) async-start(), calls=%async_computation.4 | async-start | bytes 6488064 | tf_op jit(solution)/shard_map/all_gather | solution.py:38
  7.3 492.4 %all-reduce.5.cloned.1.call-start = ((), (), s32[]{:S(2)}) async-start(), calls=%async_computation | async-start | bytes 2097152 | tf_op jit(solution)/shard_map/psum | solution.py:17
  178.2 7.7 copy-start.2
  178.2 8.4 copy-start.3
  178.2 12.8 copy-start.1
  184.0 6.9 collective-permute-start
  192.6 641.5 %all-reduce.7.cloned.1.call-start = ((), (), s32[]{:S(2)}) async-start(), calls=%async_computation.1 | async-start | bytes 2097152 | tf_op jit(solution)/shard_map/psum | solution.py:17
  502.1 22.5 %collective-permute-start.1 = (bf16[4096,128]{0,1:T(8,128)(2,1)S(1)}, bf16[4096,128]{0,1:T(8,128)(2,1)S(1)}, u32[]{:S(2)}, u32[]{:S(2)}) collective-permute-start(bf16[4096,128]{0,1:T(8,128)(2,1)S(1)} %fusion.17), channel_id=1, source_target_pairs={{0,64},{32,96},{64,0},{96,32},{128,192},{160,224},{192,128},{224,1... | collective-permute-start | bytes 3145736 | tf_op jit(solution)/shard_map/ppermute | solution.py:12
  526.2 635.3 %all-reduce.9.cloned.1.call-start = ((), (), s32[]{:S(2)}) async-start(), calls=%async_computation.2 | async-start | bytes 2097152 | tf_op jit(solution)/shard_map/psum | solution.py:17
  836.5 16.7 %collective-permute-start.2 = (bf16[4096,128]{0,1:T(8,128)(2,1)S(1)}, bf16[4096,128]{0,1:T(8,128)(2,1)S(1)}, u32[]{:S(2)}, u32[]{:S(2)}) collective-permute-start(bf16[4096,128]{0,1:T(8,128)(2,1)S(1)} %fusion.18), channel_id=1, source_target_pairs={{0,128},{32,160},{64,192},{96,224},{128,0},{160,32},{192,64},{224,... | collective-permute-start | bytes 3145736 | tf_op jit(solution)/shard_map/ppermute | solution.py:12
  854.8 635.6 %all-reduce.11.cloned.1.call-start = ((), (), s32[]{:S(2)}) async-start(), calls=%async_computation.3 | async-start | bytes 2097152 | tf_op jit(solution)/shard_map/psum | solution.py:17
  1163.9 18.2 %collective-permute-start.3 = (bf16[4096,128]{0,1:T(8,128)(2,1)S(1)}, bf16[4096,128]{0,1:T(8,128)(2,1)S(1)}, u32[]{:S(2)}, u32[]{:S(2)}) collective-permute-start(bf16[4096,128]{0,1:T(8,128)(2,1)S(1)} %fusion.19), channel_id=1, source_target_pairs={{0,256},{32,288},{64,320},{96,352},{128,384},{160,416},{192,448},{... | collective-permute-start | bytes 3145736 | tf_op jit(solution)/shard_map/ppermute | solution.py:12
Sparse Core Ops, SparseCore 0:
  9.4 168.7 all-gather.2
  192.7 306.9 all-reduce.4
  526.3 307.6 all-reduce.6
  854.9 306.5 all-reduce.8
  1183.8 306.5 all-reduce.10
where the time goes:
time: 1500 us
  waiting for transfers between devices  1430 us (95%)
  matrix products  21 us (1%)
  between operations  18.4 us (1%)
  other arithmetic  16.3 us (1%)
    psum x4, waiting for transfers between devices, broadcast(): return lax.psum(jnp.where(mine, x, jnp.zeros_like(x)), axis)  1220 us
    all_gather x1, waiting for transfers between devices, shards(): lax.all_gather(lower_panel[0], 'col', axis=0, tiled=True)  170 us
    ppermute x4, waiting for transfers between devices, from_partner(): return lax.ppermute(value, axis, pairs)  41.4 us
  transfers between devices with their start and end apart: 9, of which 8 were waited for; matrix products, arithmetic and copies ran while one was open for 1% of the time, Pallas kernels for 0%

commit v1 on v0

--- a/solution.py
+++ b/solution.py
@@ -14,7 +14,11 @@
 
 def broadcast(x, axis, root):
     mine = lax.axis_index(axis) == root
-    return lax.psum(jnp.where(mine, x, jnp.zeros_like(x)), axis)
+
+    def compute_sample_for(my_tile):
+        return lax.all_gather(my_tile, axis).sum(axis=0)
+
+    return compute_sample_for(jnp.where(mine, x, jnp.zeros_like(x)))
 
 
 def shards(lower_panel, upper_panel, diag_inverse, pivot_inverse, pattern, col_order, sep_blocks):

time: 1500 us -> 1830 us (1.22)
  the two profiles are of different devices: /device:TPU:2 before, /device:TPU:1 now
where the time goes in v1:
time: 1830 us
  waiting for transfers between devices  1690 us (92%)
  other arithmetic  64.7 us (4%)
  starting transfers between devices  36 us (2%)
  matrix products  18.4 us (1%)
    all_gather x4, waiting for transfers between devices, compute_sample_for(): return lax.all_gather(my_tile, axis).sum(axis=0)  1450 us
    all_gather x1, waiting for transfers between devices, shards(): lax.all_gather(lower_panel[0], 'col', axis=0, tiled=True)  150 us
    ppermute x4, waiting for transfers between devices, from_partner(): return lax.ppermute(value, axis, pairs)  90.9 us
    reduce_sum x4, other arithmetic, compute_sample_for(): return lax.all_gather(my_tile, axis).sum(axis=0)  48.8 us
  transfers between devices with their start and end apart: 9, of which 8 were waited for; matrix products, arithmetic and copies ran while one was open for 1% of the time, Pallas kernels for 0%

profile of v1, /device:TPU:1, one launch (start us, length us, event | category | flops | bytes accessed | tf_op | source)
XLA Modules:
  0.0 1833.0 jit_solution(11210634963639540400)
XLA Ops:
  8.2 150.3 %all-gather.11.cloned.1.call-done = bf16[1,4096,768]{2,1,0:T(8,128)(2,1)} async-done(((bf16[1,128,768]{2,1,0:T(8,128)(2,1)}), bf16[1,4096,768]{2,1,0:T(8,128)(2,1)}) %all-gather.11.cloned.1.call-update) | async-done | bytes 6291472 | tf_op jit(solution)/shard_map/all_gather | solution.py:42
  158.5 5.8 fusion.24
  164.3 23.1 %collective-permute-start = (bf16[4096,128]{0,1:T(8,128)(2,1)S(1)}, bf16[4096,128]{0,1:T(8,128)(2,1)S(1)}, u32[]{:S(2)}, u32[]{:S(2)}) collective-permute-start(bf16[4096,128]{0,1:T(8,128)(2,1)S(1)} %fusion.24), channel_id=1, source_target_pairs={{0,32},{32,0},{64,96},{96,64},{128,160},{160,128},{192,224},{224,1... | collective-permute-start | bytes 3145736 | tf_op jit(solution)/shard_map/ppermute | solution.py:12
  188.1 3.2 fusion.63
  195.3 1.6 convert_add_fusion.3
  196.8 361.3 %all-gather.13.cloned.1.call-done = bf16[131072,128]{1,0:T(8,128)(2,1)} async-done(((bf16[4096,128]{1,0:T(8,128)(2,1)}), bf16[131072,128]{1,0:T(8,128)(2,1)}) %all-gather.13.cloned.1.call-update) | async-done | bytes 33554448 | tf_op jit(solution)/shard_map/all_gather | solution.py:19
  558.1 12.5 reduce_sum.88
  570.6 1.7 fusion.17
  572.4 5.0 collective-permute-start.1
  578.0 46.8 %collective-permute-done.1 = bf16[4096,128]{0,1:T(8,128)(2,1)S(1)} collective-permute-done((bf16[4096,128]{0,1:T(8,128)(2,1)S(1)}, bf16[4096,128]{0,1:T(8,128)(2,1)S(1)}, u32[]{:S(2)}, u32[]{:S(2)}) %collective-permute-start.1) | collective-permute-done | bytes 1048608 | tf_op jit(solution)/shard_map/ppermute | solution.py:12
  624.7 1.6 fusion.21
  629.8 363.6 %all-gather.15.cloned.1.call-done = bf16[131072,128]{1,0:T(8,128)(2,1)} async-done(((bf16[4096,128]{1,0:T(8,128)(2,1)}), bf16[131072,128]{1,0:T(8,128)(2,1)}) %all-gather.15.cloned.1.call-update) | async-done | bytes 33554448 | tf_op jit(solution)/shard_map/all_gather | solution.py:19
  993.3 12.4 reduce_sum.89
  1005.7 1.7 fusion.18
  1007.4 3.1 collective-permute-start.2
  1011.1 22.1 %collective-permute-done.2 = bf16[4096,128]{0,1:T(8,128)(2,1)S(1)} collective-permute-done((bf16[4096,128]{0,1:T(8,128)(2,1)S(1)}, bf16[4096,128]{0,1:T(8,128)(2,1)S(1)}, u32[]{:S(2)}, u32[]{:S(2)}) %collective-permute-start.2) | collective-permute-done | bytes 1048608 | tf_op jit(solution)/shard_map/ppermute | solution.py:12
  1033.2 1.6 fusion.22
  1038.3 363.6 %all-gather.17.cloned.1.call-done = bf16[131072,128]{1,0:T(8,128)(2,1)} async-done(((bf16[4096,128]{1,0:T(8,128)(2,1)}), bf16[131072,128]{1,0:T(8,128)(2,1)}) %all-gather.17.cloned.1.call-update) | async-done | bytes 33554448 | tf_op jit(solution)/shard_map/all_gather | solution.py:19
  1401.9 12.4 reduce_sum.90
  1414.3 1.7 fusion.19
  1416.0 4.6 collective-permute-start.3
  1421.2 22.1 %collective-permute-done.3 = bf16[4096,128]{0,1:T(8,128)(2,1)S(1)} collective-permute-done((bf16[4096,128]{0,1:T(8,128)(2,1)S(1)}, bf16[4096,128]{0,1:T(8,128)(2,1)S(1)}, u32[]{:S(2)}, u32[]{:S(2)}) %collective-permute-start.3) | collective-permute-done | bytes 1048608 | tf_op jit(solution)/shard_map/ppermute | solution.py:12
  1448.3 363.6 %all-gather.19.cloned.1.call-done = bf16[131072,128]{1,0:T(8,128)(2,1)} async-done(((bf16[4096,128]{1,0:T(8,128)(2,1)}), bf16[131072,128]{1,0:T(8,128)(2,1)}) %all-gather.19.cloned.1.call-update) | async-done | bytes 33554448 | tf_op jit(solution)/shard_map/all_gather | solution.py:19
  1811.9 11.5 reduce_sum.91
  (48 shorter events, 18.1 us)
Async XLA Ops:
  6.5 152.0 %copy-start = (bf16[1,1,768,768]{3,2,1,0:T(8,128)(2,1)S(1)}, bf16[1,1,768,768]{3,2,1,0:T(8,128)(2,1)}, u32[]{:S(2)}) copy-start(bf16[1,1,768,768]{3,2,1,0:T(8,128)(2,1)} %param.9) | copy-start | bytes 3538948
  6.5 152.0 %all-gather.11.cloned.1.call-start = ((), (), s32[]{:S(2)}) async-start(), calls=%async_computation | async-start | bytes 6488064 | tf_op jit(solution)/shard_map/all_gather | solution.py:42
  7.3 550.9 %all-gather.13.cloned.1.call-start = ((), (), s32[]{:S(2)}) async-start(), calls=%async_computation.1 | async-start | bytes 34603008 | tf_op jit(solution)/shard_map/all_gather | solution.py:19
  158.5 28.9 %copy-start.6 = (s32[4]{0:T(128)S(1)}, s32[4]{0:T(128)}, u32[]{:S(2)}) copy-start(s32[4]{0:T(128)} %param.13) | copy-start | bytes 52
  158.5 29.6 %copy-start.7 = (s32[32]{0:T(128)S(1)}, s32[32]{0:T(128)}, u32[]{:S(2)}) copy-start(s32[32]{0:T(128)} %param.12) | copy-start | bytes 388
  158.5 33.4 %copy-start.5 = (bf16[4,128,128]{2,1,0:T(8,128)(2,1)S(1)}, bf16[4,128,128]{2,1,0:T(8,128)(2,1)}, u32[]{:S(2)}) copy-start(bf16[4,128,128]{2,1,0:T(8,128)(2,1)} %param.10) | copy-start | bytes 393220
  164.3 27.6 %collective-permute-start = (bf16[4096,128]{0,1:T(8,128)(2,1)S(1)}, bf16[4096,128]{0,1:T(8,128)(2,1)S(1)}, u32[]{:S(2)}, u32[]{:S(2)}) collective-permute-start(bf16[4096,128]{0,1:T(8,128)(2,1)S(1)} %fusion.24), channel_id=1, source_target_pairs={{0,32},{32,0},{64,96},{96,64},{128,160},{160,128},{192,224},{224,1... | collective-permute-start | bytes 3145736 | tf_op jit(solution)/shard_map/ppermute | solution.py:12
  193.5 799.8 %all-gather.15.cloned.1.call-start = ((), (), s32[]{:S(2)}) async-start(), calls=%async_computation.2 | async-start | bytes 34603008 | tf_op jit(solution)/shard_map/all_gather | solution.py:19
  558.1 12.5 copy-start.2
  572.4 52.4 %collective-permute-start.1 = (bf16[4096,128]{0,1:T(8,128)(2,1)S(1)}, bf16[4096,128]{0,1:T(8,128)(2,1)S(1)}, u32[]{:S(2)}, u32[]{:S(2)}) collective-permute-start(bf16[4096,128]{0,1:T(8,128)(2,1)S(1)} %fusion.17), channel_id=1, source_target_pairs={{0,64},{32,96},{64,0},{96,32},{128,192},{160,224},{192,128},{224,1... | collective-permute-start | bytes 3145736 | tf_op jit(solution)/shard_map/ppermute | solution.py:12
  624.7 1.6 copy-start.3
  626.3 775.5 %all-gather.17.cloned.1.call-start = ((), (), s32[]{:S(2)}) async-start(), calls=%async_computation.3 | async-start | bytes 34603008 | tf_op jit(solution)/shard_map/all_gather | solution.py:19
  1007.4 25.8 %collective-permute-start.2 = (bf16[4096,128]{0,1:T(8,128)(2,1)S(1)}, bf16[4096,128]{0,1:T(8,128)(2,1)S(1)}, u32[]{:S(2)}, u32[]{:S(2)}) collective-permute-start(bf16[4096,128]{0,1:T(8,128)(2,1)S(1)} %fusion.18), channel_id=1, source_target_pairs={{0,128},{32,160},{64,192},{96,224},{128,0},{160,32},{192,64},{224,... | collective-permute-start | bytes 3145736 | tf_op jit(solution)/shard_map/ppermute | solution.py:12
  1033.2 1.6 copy-start.4
  1034.8 777.1 %all-gather.19.cloned.1.call-start = ((), (), s32[]{:S(2)}) async-start(), calls=%async_computation.4 | async-start | bytes 34603008 | tf_op jit(solution)/shard_map/all_gather | solution.py:19
  1416.0 27.3 %collective-permute-start.3 = (bf16[4096,128]{0,1:T(8,128)(2,1)S(1)}, bf16[4096,128]{0,1:T(8,128)(2,1)S(1)}, u32[]{:S(2)}, u32[]{:S(2)}) collective-permute-start(bf16[4096,128]{0,1:T(8,128)(2,1)S(1)} %fusion.19), channel_id=1, source_target_pairs={{0,256},{32,288},{64,320},{96,352},{128,384},{160,416},{192,448},{... | collective-permute-start | bytes 3145736 | tf_op jit(solution)/shard_map/ppermute | solution.py:12
  1811.9 14.5 copy-start.1
Sparse Core Ops, SparseCore 0:
  9.4 149.0 all-gather.10
  193.6 364.5 all-gather.12
  626.5 366.8 all-gather.14
  1034.9 366.9 all-gather.16
  1444.9 366.9 all-gather.18
